TPU v7x, 32 devices: a whole 2x2x4 slice. The times are simulated.
32 devices in a mesh: sens: 2 (over x), sx: 4 (over z), sy: 4 (over y, core).
Axes of the slice: x: 2, y: 2, z: 4, core: 2. Of those that a mesh axis runs over, the one named last changes fastest.
Arguments:
- records: bfloat16 [4, 128, 128], P(None, 'sens'), may hold values from -6 to 6
- kernel: bfloat16 [128, 64, 32, 128], P('sens', 'sx', 'sy'), may hold values from -0.09375 to 0.09375
- diffusion: float32 [64, 32], P('sx', 'sy'), may hold values from 0.04 to 0.24
Outputs:
- predicted: float32 [4, 128, 128], P(None, ('sens', 'sx', 'sy'))
All inputs are finite; a program needn't handle non-finite values.
Results may differ from a plain program's by a relative error of at most 0.0011.
Values may be sent and summed in bfloat16 or wider, within the bound.
A program may use at most 64 MiB of HBM per device.

v0:
```python
import jax
import jax.numpy as jnp
from jax import lax
from jax.sharding import PartitionSpec as P

SWEEPS = 4


def extended(shard, sides, width):
    for axis, dim in sides:
        count, length = (lax.axis_size(axis), shard.shape[dim])
        up = [(i, (i + 1) % count) for i in range(count - 1)]
        down = [(j, i) for i, j in up]
        last = lax.slice_in_dim(shard, length - width, length, axis=dim)
        first = lax.slice_in_dim(shard, 0, width, axis=dim)
        before = lax.ppermute(last, axis, up)
        after = lax.ppermute(first, axis, down)
        shard = jnp.concatenate([before, shard, after], axis=dim)
    return shard


def neighbours(padded):
    return padded[:, 2:, 1:-1] + padded[:, :-2, 1:-1] + padded[:, 1:-1, 2:] + padded[:, 1:-1, :-2]


def smooth(prior_field, diffusion):
    weights = diffusion[None, :, :, None]
    margin = SWEEPS
    padded, rate_wide = (
        extended(prior_field, (("sx", 1), ("sy", 2)), margin),
        extended(weights, (("sx", 1), ("sy", 2)), margin),
    )
    for repeat in range(margin):
        interior = padded[:, 1:-1, 1:-1]
        rate_wide = rate_wide[:, 1:-1, 1:-1]
        padded = interior + rate_wide * (neighbours(padded) - 4.0 * interior)
    return padded


def per_device(records, kernel, diffusion):
    vectors, sensors, window = records.shape
    cells_x, cells_y = diffusion.shape
    kernel_rows = kernel.reshape(kernel.shape[0], cells_x * cells_y, window)
    partials = lax.conv_general_dilated(
        records,
        kernel_rows,
        (1,),
        [(0, window - 1)],
        dimension_numbers=("NCH", "IOH", "NCH"),
        preferred_element_type=jnp.float32,
    )
    partials = partials.reshape(vectors, cells_x, cells_y, window)
    whole_sum = lax.psum(partials, "sens")
    smoothed = smooth(whole_sum, diffusion).astype(jnp.bfloat16)
    flipped = smoothed.reshape(vectors, cells_x * cells_y, window)[:, :, ::-1]
    backward = lax.conv_general_dilated(
        flipped,
        kernel_rows,
        (1,),
        [(0, window - 1)],
        dimension_numbers=("NCH", "OIH", "NCH"),
        preferred_element_type=jnp.float32,
    )
    summands = backward[:, :, ::-1]
    return lax.psum_scatter(summands, ("sx", "sy"), scatter_dimension=1, tiled=True)


def solution(mesh):
    return jax.shard_map(
        per_device,
        mesh=mesh,
        in_specs=(P(None, "sens", None), P("sens", "sx", "sy", None), P("sx", "sy")),
        out_specs=P(None, ("sens", "sx", "sy"), None),
        check_vma=False,
    )
```

profile of v0, /device:TPU:0, one launch (start us, length us, event | category | flops | bytes accessed | tf_op | source)
XLA Modules:
  0.0 174.8 jit_solution(15188670381473331746)
XLA Ops:
  6.5 0.0 all-reduce.4.cloned.1.call-start
  6.5 0.8 fusion.17
  7.4 1.3 collective-permute-start.5
  8.7 5.6 %collective-permute-start.4 = (f32[1,4,8,1]{1,2,3,0:T(8,128)S(1)}, f32[1,4,8,1]{1,2,3,0:T(8,128)S(1)}, u32[]{:S(2)}, u32[]{:S(2)}) collective-permute-start(f32[1,4,8,1]{1,2,3,0:T(8,128)S(1)} %get-tuple-element.11), channel_id=1, source_target_pairs={{0,4},{4,8},{8,12},{1,5},{5,9},{9,13},{2,6},{6,10},{10,14},{3,7},{... | collective-permute-start | bytes 392 | tf_op jit(solution)/shard_map/ppermute | solution.py:16
  14.3 1.0 copy.22
  15.2 0.0 copy-start
  15.2 3.3 %copy.23 = bf16[64,128,128]{1,0,2:T(8,128)(2,1)S(1)} copy(bf16[64,128,128]{2,1,0:T(8,128)(2,1)} %bitcast.16) | data formatting | bytes 4194304 | tf_op jit(solution)/shard_map/reshape | solution.py:43
  18.5 0.0 collective-permute-done.5
  18.6 0.0 collective-permute-done.4
  18.6 0.0 copy-done
  18.6 0.1 pad_maximum_fusion.2
  18.7 1.3 collective-permute-start.7
  19.9 3.0 %collective-permute-start.6 = (f32[1,24,4,1]{1,2,3,0:T(4,128)S(1)}, f32[1,24,4,1]{1,2,3,0:T(4,128)S(1)}, u32[]{:S(2)}, u32[]{:S(2)}) collective-permute-start(f32[1,24,4,1]{1,2,3,0:T(4,128)S(1)} %get-tuple-element.9), channel_id=1, source_target_pairs={{0,1},{1,2},{2,3},{4,5},{5,6},{6,7},{8,9},{9,10},{10,11},{12,13},{... | collective-permute-start | bytes 1160 | tf_op jit(solution)/shard_map/ppermute | solution.py:16
  23.0 2.9 %fusion.18 = f32[4,128,128]{1,0,2:T(4,128)S(1)} fusion(bf16[4,64,128]{1,0,2:T(4,128)(2,1)S(1)} %copy.22, bf16[64,128,128]{1,0,2:T(8,128)(2,1)S(1)} %copy.23), kind=kOutput, calls=%fused_computation.40 | convolution fusion | flops 541065216 | bytes 2424832 | tf_op jit(solution)/shard_map/conv_general_dilated | solution.py:44
  25.9 0.8 copy.24
  26.8 0.0 all-reduce.4.cloned.1.call-update
  26.8 0.0 all-reduce.6.cloned.1.call-start
  26.9 0.1 copy.28
  26.9 0.0 collective-permute-done.7
  26.9 0.0 collective-permute-done.6
  26.9 0.1 pad_maximum_fusion.1
  27.0 0.1 slice_bitcast_fusion.2
  27.1 23.8 %all-reduce.4.cloned.1.call-done = f32[4,16,8,128]{3,2,1,0:T(8,128)} async-done(((f32[4,16,8,128]{3,2,1,0:T(8,128)}), f32[4,16,8,128]{3,2,1,0:T(8,128)}) %all-reduce.4.cloned.1.call-update) | async-done | bytes 262160 | tf_op jit(solution)/shard_map/psum | solution.py:53
  50.9 0.9 fusion.15
  51.8 3.4 %collective-permute-start = (f32[4,4,8,128]{3,2,1,0:T(8,128)S(1)}, f32[4,4,8,128]{3,2,1,0:T(8,128)S(1)}, u32[]{:S(2)}, u32[]{:S(2)}) collective-permute-start(f32[4,4,8,128]{3,2,1,0:T(8,128)S(1)} %get-tuple-element.8), channel_id=1, source_target_pairs={{0,4},{4,8},{8,12},{1,5},{5,9},{9,13},{2,6},{6,10},{10,14},{3,7},{... | collective-permute-start | bytes 196616 | tf_op jit(solution)/shard_map/ppermute | solution.py:16
  55.2 0.1 slice_bitcast_fusion.1
  55.3 0.1 copy.25
  55.4 0.1 copy.26
  55.5 1.3 collective-permute-start.1
  56.8 0.3 collective-permute-done
  57.1 1.0 constant_dynamic-update-slice_fusion.1
  58.1 3.6 %collective-permute-done.1 = f32[4,4,8,128]{3,2,1,0:T(8,128)S(1)} collective-permute-done((f32[4,4,8,128]{3,2,1,0:T(8,128)S(1)}, f32[4,4,8,128]{3,2,1,0:T(8,128)S(1)}, u32[]{:S(2)}, u32[]{:S(2)}) %collective-permute-start.1) | collective-permute-done | bytes 65568 | tf_op jit(solution)/shard_map/ppermute | solution.py:17
  61.6 0.1 fusion.14
  61.7 1.3 collective-permute-start.3
  63.0 3.0 %collective-permute-start.2 = (f32[4,24,4,128]{3,2,1,0:T(4,128)S(1)}, f32[4,24,4,128]{3,2,1,0:T(4,128)S(1)}, u32[]{:S(2)}, u32[]{:S(2)}) collective-permute-start(f32[4,24,4,128]{3,2,1,0:T(4,128)S(1)} %get-tuple-element.5), channel_id=1, source_target_pairs={{0,1},{1,2},{2,3},{4,5},{5,6},{6,7},{8,9},{9,10},{10,11},{12,13},{... | collective-permute-start | bytes 589832 | tf_op jit(solution)/shard_map/ppermute | solution.py:16
  66.1 0.1 slice_bitcast_fusion
  66.1 0.1 copy.27
  66.2 0.0 collective-permute-done.3
  66.2 0.9 collective-permute-done.2
  67.1 0.2 pad_maximum_fusion
  67.2 0.3 fusion.2
  67.5 0.2 fusion.5
  67.8 0.2 fusion.8
  68.0 0.1 fusion.13
  68.1 0.0 copy-start.1
  68.2 0.4 rev.6
  68.6 0.1 copy.29
  68.7 6.1 %fusion.19 = f32[4,64,128]{1,0,2:T(4,128)S(1)} fusion(bf16[4,128,128]{1,0,2:T(4,128)(2,1)S(1)} %copy.29, bf16[64,128,128]{1,0,2:T(8,128)(2,1)S(1)} %copy.23), kind=kOutput, calls=%fused_computation.41 | convolution fusion | flops 541065216 | bytes 2359296 | tf_op jit(solution)/shard_map/conv_general_dilated | solution.py:56
  74.9 0.8 copy.31
  75.7 0.0 all-reduce.6.cloned.1.call-update
  75.7 0.0 copy-done.1
  75.7 0.6 dynamic-slice
  77.0 89.7 %all-reduce.6.cloned.1.call-done = f32[4,64,128]{2,0,1:T(4,128)} async-done(((f32[4,64,128]{2,0,1:T(4,128)}), f32[4,64,128]{2,0,1:T(4,128)}) %all-reduce.6.cloned.1.call-update) | async-done | bytes 131088
  166.7 0.7 constant_dynamic-slice_fusion
  167.4 0.6 copy.32
  (4 shorter events, 0.1 us)
Async XLA Ops:
  6.5 44.4 %all-reduce.4.cloned.1.call-start = ((), (), s32[]{:S(2)}) async-start(), calls=%async_computation | async-start | bytes 524288 | tf_op jit(solution)/shard_map/psum | solution.py:53
  7.4 11.2 %collective-permute-start.5 = (f32[1,4,8,1]{1,2,3,0:T(8,128)S(1)}, f32[1,4,8,1]{1,2,3,0:T(8,128)S(1)}, u32[]{:S(2)}, u32[]{:S(2)}) collective-permute-start(f32[1,4,8,1]{1,2,3,0:T(8,128)S(1)} %get-tuple-element.12), channel_id=1, source_target_pairs={{4,0},{8,4},{12,8},{5,1},{9,5},{13,9},{6,2},{10,6},{14,10},{7,3},{... | collective-permute-start | bytes 392 | tf_op jit(solution)/shard_map/ppermute | solution.py:17
  8.7 9.9 %collective-permute-start.4 = (f32[1,4,8,1]{1,2,3,0:T(8,128)S(1)}, f32[1,4,8,1]{1,2,3,0:T(8,128)S(1)}, u32[]{:S(2)}, u32[]{:S(2)}) collective-permute-start(f32[1,4,8,1]{1,2,3,0:T(8,128)S(1)} %get-tuple-element.11), channel_id=1, source_target_pairs={{0,4},{4,8},{8,12},{1,5},{5,9},{9,13},{2,6},{6,10},{10,14},{3,7},{... | collective-permute-start | bytes 392 | tf_op jit(solution)/shard_map/ppermute | solution.py:16
  15.2 3.3 %copy-start = (f32[16,8]{0,1:T(8,128)S(1)}, f32[16,8]{0,1:T(8,128)}, u32[]{:S(2)}) copy-start(f32[16,8]{0,1:T(8,128)} %param.5) | copy-start | bytes 1540
  18.7 8.3 %collective-permute-start.7 = (f32[1,24,4,1]{1,2,3,0:T(4,128)S(1)}, f32[1,24,4,1]{1,2,3,0:T(4,128)S(1)}, u32[]{:S(2)}, u32[]{:S(2)}) collective-permute-start(f32[1,24,4,1]{1,2,3,0:T(4,128)S(1)} %get-tuple-element.10), channel_id=1, source_target_pairs={{1,0},{2,1},{3,2},{5,4},{6,5},{7,6},{9,8},{10,9},{11,10},{13,12},{... | collective-permute-start | bytes 1160 | tf_op jit(solution)/shard_map/ppermute | solution.py:17
  19.9 7.0 %collective-permute-start.6 = (f32[1,24,4,1]{1,2,3,0:T(4,128)S(1)}, f32[1,24,4,1]{1,2,3,0:T(4,128)S(1)}, u32[]{:S(2)}, u32[]{:S(2)}) collective-permute-start(f32[1,24,4,1]{1,2,3,0:T(4,128)S(1)} %get-tuple-element.9), channel_id=1, source_target_pairs={{0,1},{1,2},{2,3},{4,5},{5,6},{6,7},{8,9},{9,10},{10,11},{12,13},{... | collective-permute-start | bytes 1160 | tf_op jit(solution)/shard_map/ppermute | solution.py:16
  26.8 139.9 %all-reduce.6.cloned.1.call-start = ((), (), s32[]{:S(2)}) async-start(), calls=%async_computation.1 | async-start | bytes 262144
  51.8 5.3 %collective-permute-start = (f32[4,4,8,128]{3,2,1,0:T(8,128)S(1)}, f32[4,4,8,128]{3,2,1,0:T(8,128)S(1)}, u32[]{:S(2)}, u32[]{:S(2)}) collective-permute-start(f32[4,4,8,128]{3,2,1,0:T(8,128)S(1)} %get-tuple-element.8), channel_id=1, source_target_pairs={{0,4},{4,8},{8,12},{1,5},{5,9},{9,13},{2,6},{6,10},{10,14},{3,7},{... | collective-permute-start | bytes 196616 | tf_op jit(solution)/shard_map/ppermute | solution.py:16
  55.5 6.1 %collective-permute-start.1 = (f32[4,4,8,128]{3,2,1,0:T(8,128)S(1)}, f32[4,4,8,128]{3,2,1,0:T(8,128)S(1)}, u32[]{:S(2)}, u32[]{:S(2)}) collective-permute-start(f32[4,4,8,128]{3,2,1,0:T(8,128)S(1)} %get-tuple-element.7), channel_id=1, source_target_pairs={{4,0},{8,4},{12,8},{5,1},{9,5},{13,9},{6,2},{10,6},{14,10},{7,3},{... | collective-permute-start | bytes 196616 | tf_op jit(solution)/shard_map/ppermute | solution.py:17
  61.7 4.5 %collective-permute-start.3 = (f32[4,24,4,128]{3,2,1,0:T(4,128)S(1)}, f32[4,24,4,128]{3,2,1,0:T(4,128)S(1)}, u32[]{:S(2)}, u32[]{:S(2)}) collective-permute-start(f32[4,24,4,128]{3,2,1,0:T(4,128)S(1)} %get-tuple-element.6), channel_id=1, source_target_pairs={{1,0},{2,1},{3,2},{5,4},{6,5},{7,6},{9,8},{10,9},{11,10},{13,12},{... | collective-permute-start | bytes 589832 | tf_op jit(solution)/shard_map/ppermute | solution.py:17
  63.0 4.1 %collective-permute-start.2 = (f32[4,24,4,128]{3,2,1,0:T(4,128)S(1)}, f32[4,24,4,128]{3,2,1,0:T(4,128)S(1)}, u32[]{:S(2)}, u32[]{:S(2)}) collective-permute-start(f32[4,24,4,128]{3,2,1,0:T(4,128)S(1)} %get-tuple-element.5), channel_id=1, source_target_pairs={{0,1},{1,2},{2,3},{4,5},{5,6},{6,7},{8,9},{9,10},{10,11},{12,13},{... | collective-permute-start | bytes 589832 | tf_op jit(solution)/shard_map/ppermute | solution.py:16
  68.1 7.6 %copy-start.1 = (u32[32]{0:T(128)S(1)}, u32[32]{0:T(128)}, u32[]{:S(2)}) copy-start(u32[32]{0:T(128)} %constant.3) | copy-start | bytes 388
Sparse Core Ops, SparseCore 0:
  26.9 23.9 all-reduce.3
  75.8 90.8 all-reduce.5
where the time goes:
time: 176 us; the launch traced here: 175 us
  waiting for transfers between devices  118 us (67%)
  starting transfers between devices  20.2 us (11%)
  between operations  14.3 us (8%)
  local copies, waits for them, and re-layouts  11.7 us (7%)
  matrix products  9.07 us (5%)
    unnamed x3, waiting for transfers between devices  89.8 us
    psum x1, waiting for transfers between devices, per_device(): whole_sum = lax.psum(partials, 'sens')  23.8 us
    ppermute x4, starting transfers between devices, extended(): before = lax.ppermute(last, axis, up)  15.1 us
    conv_general_dilated x1, matrix products, per_device(): lax.conv_general_dilated(flipped, kernel_rows, (1,), [(0, window - 1)], d...  6.13 us
    ppermute x4, starting transfers between devices, extended(): after = lax.ppermute(first, axis, down)  5.14 us
    ppermute x4, waiting for transfers between devices, extended(): after = lax.ppermute(first, axis, down)  3.56 us
  transfers between devices with their start and end apart: 10, of which 5 were waited for; matrix products, arithmetic and copies ran while one was open for 6% of the time, Pallas kernels for 0%

commit v1 on v0

v1 whole, which is shorter than its diff:
```python
import functools

import jax
import jax.numpy as jnp
from jax import lax
from jax.experimental import pallas as pl
from jax.experimental.pallas import tpu as pltpu
from jax.sharding import PartitionSpec as P

SWEEPS = 4
MESH = pl.DeviceIdType.MESH
F32 = jnp.float32
BF16 = jnp.bfloat16
DIRECTIONS = ((-1, 0), (1, 0), (0, -1), (0, 1), (-1, -1), (-1, 1), (1, -1), (1, 1))


def opposite(d):
    dx, dy = DIRECTIONS[d]
    return DIRECTIONS.index((-dx, -dy))


def lane_iota(rows, window):
    return lax.broadcasted_iota(jnp.int32, (rows, window), 1)


def row_iota(rows, window):
    return lax.broadcasted_iota(jnp.int32, (rows, window), 0)


class Halo:
    def __init__(self, sizes, cells_x, cells_y, margin):
        self.nx, self.ny = sizes
        self.cx, self.cy, self.m = cells_x, cells_y, margin
        half = margin // 2
        low = list(range(half))
        high = [cells_x - margin + i for i in low]
        middle = [i for i in range(margin, cells_x - margin)]
        mid = len(middle) // 2
        self.first = low + high + middle[:mid]
        self.second = [i + half for i in low + high] + middle[mid:]
        self.pairs = len(self.first)
        self.half = half
        self.mx, self.my = lax.axis_index("sx"), lax.axis_index("sy")

    def exists(self, d):
        dx, dy = DIRECTIONS[d]
        ok = jnp.bool_(True)
        if dx:
            ok = ok & (self.mx + dx >= 0) & (self.mx + dx < self.nx)
        if dy:
            ok = ok & (self.my + dy >= 0) & (self.my + dy < self.ny)
        return ok

    def pack(self, centre, packed, fields):
        rows = row_iota(self.cy, centre.shape[-1])
        upper = rows < self.cy // 2
        for f in range(fields):
            for i, (a, b) in enumerate(zip(self.first, self.second)):
                one, two = centre[f, a], pltpu.roll(centre[f, b], self.cy // 2, 0)
                packed[0, f, i] = jnp.where(upper, one, two)
                packed[1, f, i] = jnp.where(upper, two, one)

    def copy(self, d, centre, packed, x_got, y_got, send_sem, recv_sem):
        dx, dy = DIRECTIONS[d]
        o = opposite(d)
        if dy == 0:
            start = 0 if dx < 0 else self.cx - self.m
            src = centre.at[:, pl.ds(start, self.m)]
            dst = x_got.at[0 if dx > 0 else 1]
        else:
            side = packed.at[0 if dy < 0 else 1]
            place = y_got.at[1 if dy < 0 else 0]
            if dx == 0:
                src, dst = side, place.at[:, pl.ds(self.half, self.pairs)]
            else:
                src = side.at[:, pl.ds(0 if dx < 0 else self.half, self.half)]
                dst = place.at[:, pl.ds(0 if dx > 0 else self.half + self.pairs, self.half)]
        return pltpu.make_async_remote_copy(
            src_ref=src, dst_ref=dst, send_sem=send_sem.at[d], recv_sem=recv_sem.at[o],
            device_id={"sx": self.mx + dx, "sy": self.my + dy}, device_id_type=MESH)

    def start(self, *refs):
        for d in range(len(DIRECTIONS)):
            @pl.when(self.exists(d))
            def _():
                self.copy(d, *refs).start()

    def wait(self, *refs):
        for d in range(len(DIRECTIONS)):
            @pl.when(self.exists(d))
            def _():
                self.copy(opposite(d), *refs).wait_recv()
                self.copy(d, *refs).wait_send()

    def clear(self, x_got, y_got):
        x_got[...] = jnp.zeros_like(x_got)
        y_got[...] = jnp.zeros_like(y_got)

    def assemble(self, f, centre, x_got, y_got, wide):
        m, cx, cy = self.m, self.cx, self.cy
        wide[f, pl.ds(m, cx), pl.ds(0, cy)] = centre[f]
        wide[f, pl.ds(0, m), pl.ds(0, cy)] = x_got[0, f]
        wide[f, pl.ds(m + cx, m), pl.ds(0, cy)] = x_got[1, f]
        upper = row_iota(cy, centre.shape[-1]) < cy // 2
        half = self.half
        first = [i - m for i in range(half)] + self.first + [cx + i for i in range(half)]
        second = [i - m + half for i in range(half)] + self.second + [cx + half + i for i in range(half)]
        for i, (a, b) in enumerate(zip(first, second)):
            left, right = y_got[0, f, i], y_got[1, f, i]
            wide[f, m + a, pl.ds(cy, cy)] = jnp.where(upper, right, left)
            wide[f, m + b, pl.ds(cy, cy)] = pltpu.roll(jnp.where(upper, left, right), cy // 2, 0)


def kernel(sizes, vectors, sensors, cells_x, cells_y, window,
           records_ref, rates_ref, kernel_hbm, out_ref,
           kbuf, recf, toep, part, got, field, packed, x_got, y_got, wide,
           d_packed, d_x_got, d_y_got, d_wide, smooth_t, pred, pred_got,
           k_sem, s_send, s_recv, h_send, h_recv, d_send, d_recv, g_send, g_recv, p_send, p_recv):
    n_s, n_x, n_y = sizes
    points = cells_x * cells_y
    chunks = min(n_s, vectors)
    per = vectors // chunks
    margin = SWEEPS
    n_q = n_x * n_y
    group = sensors // n_q
    step = 8
    steps = sensors // step
    me_s, me_x, me_y = lax.axis_index("sens"), lax.axis_index("sx"), lax.axis_index("sy")
    mine = lax.rem(me_s, chunks)
    base = me_s - mine
    me_q = me_x * n_y + me_y

    def k_copy(i):
        return pltpu.make_async_copy(
            kernel_hbm.at[pl.ds(i * step, step)], kbuf.at[pl.ds(i * step, step)], k_sem.at[i])

    for i in range(steps):
        k_copy(i).start()

    halo = Halo((n_x, n_y), cells_x, cells_y, margin)
    halo.clear(x_got, y_got)
    halo.clear(d_x_got, d_y_got)

    barrier = pltpu.get_barrier_semaphore()

    def greet_tile(k, _):
        q = lax.rem(me_q + k, n_q)
        pl.semaphore_signal(barrier, inc=1, device_id={"sx": q // n_y, "sy": lax.rem(q, n_y)}, device_id_type=MESH)
        return 0

    lax.fori_loop(1, n_q, greet_tile, 0)
    for k in range(1, n_s):
        pl.semaphore_signal(barrier, inc=1, device_id={"sens": lax.rem(me_s + k, n_s)}, device_id_type=MESH)

    anti = (lane_iota(window, window) + row_iota(window, window) == window - 1).astype(BF16)
    for v in range(vectors):
        recf[v] = jnp.dot(records_ref[v], anti, preferred_element_type=F32)

    halo.pack(rates_ref, d_packed, 1)

    pack_rows = 16
    lanes16, rows16 = lane_iota(pack_rows, window), row_iota(pack_rows, window)

    def adjoint(chunk, slot, first):
        for v in range(per):
            part[slot, v] = jnp.zeros((points, window), F32)

        def body(i, _):
            if first:
                k_copy(i).wait()
            for v in range(per):
                block = recf[chunk * per + v, pl.ds(pl.multiple_of(i * step, step), step)]
                for s in range(step):
                    line = jnp.broadcast_to(block[s:s + 1], (pack_rows, window))
                    seed = pltpu.roll(line, 0, 1, stride=1, stride_axis=0)
                    seed = jnp.where(lanes16 >= rows16, seed, 0.0)
                    for j in range(window // pack_rows):
                        shifted = seed if j == 0 else jnp.where(
                            lanes16 >= j * pack_rows, pltpu.roll(seed, j * pack_rows, 1), 0.0)
                        toep[pl.ds(s * window + j * pack_rows, pack_rows), pl.ds(v * window, window)] = shifted.astype(BF16)
            lhs = jnp.concatenate([kbuf[i * step + s] for s in range(step)], axis=1)
            res = jnp.dot(lhs, toep[...], preferred_element_type=F32)
            for v in range(per):
                part[slot, v] += res[:, v * window:(v + 1) * window]
            return 0

        lax.fori_loop(0, steps, body, 0)

    def s_copy(k, hop):
        return pltpu.make_async_remote_copy(
            src_ref=part.at[k], dst_ref=got.at[hop - 1], send_sem=s_send.at[hop - 1], recv_sem=s_recv.at[hop - 1],
            device_id={"sens": lax.rem(me_s + hop, n_s)}, device_id_type=MESH)

    halo_d = (rates_ref, d_packed, d_x_got, d_y_got, d_send, d_recv)
    halo_f = (field, packed, x_got, y_got, h_send, h_recv)

    for k in range(1, chunks + 1):
        adjoint(lax.rem(me_s + k, chunks), k - 1, k == 1)
        if k == 1:
            pl.semaphore_wait(barrier, n_q - 1 + n_s - 1)
        for hop in range(k, n_s, chunks):
            s_copy(k - 1, hop).start()
        if k == 1:
            halo.start(*halo_d)

    halo.wait(*halo_d)
    halo.assemble(0, rates_ref, d_x_got, d_y_got, d_wide)

    for hop in range(1, n_s):
        s_copy((hop - 1) % chunks, hop).wait_recv()
    for v in range(per):
        total = part[chunks - 1, v]
        for hop in range(1, n_s):
            total = total + got[hop - 1, v]
        field[v] = total.reshape(cells_x, cells_y, window)
    halo.pack(field, packed, per)
    halo.start(*halo_f)
    halo.wait(*halo_f)
    wide_rows = 2 * cells_y
    for v in range(per):
        halo.assemble(v, field, x_got, y_got, wide)
        now = wide[v]
        for repeat in range(SWEEPS):
            interior = now[1:-1]
            beside = now[2:] + now[:-2] + pltpu.roll(interior, wide_rows - 1, 1) + pltpu.roll(interior, 1, 1)
            rate = d_wide[0, pl.ds(repeat + 1, cells_x + 2 * (margin - repeat - 1))]
            now = interior + rate * (beside - 4.0 * interior)
        done = now[:, :cells_y].reshape(points, window).astype(BF16)
        smooth_t[mine, pl.ds(v * window, window)] = lax.dot_general(
            anti, done, (((1,), (1,)), ((), ())), preferred_element_type=F32).astype(BF16)

    def g_copy(k):
        return pltpu.make_async_remote_copy(
            src_ref=smooth_t.at[mine], dst_ref=smooth_t.at[mine], send_sem=g_send.at[k - 1], recv_sem=g_recv.at[k - 1],
            device_id={"sens": base + lax.rem(mine + k, chunks)}, device_id_type=MESH)

    for k in range(1, chunks):
        g_copy(k).start()

    lanes8, rows8 = lane_iota(8, window), row_iota(8, window)

    def forward(chunk, send):
        def body(i, _):
            q = lax.rem(me_q + 1 + i, n_q)
            rhs = jnp.concatenate([kbuf[q * group + s] for s in range(group)], axis=1)
            res = jnp.dot(smooth_t[chunk], rhs, preferred_element_type=F32)
            lines = []
            for v in range(per):
                for s in range(group):
                    tile = res[v * window:(v + 1) * window, s * window:(s + 1) * window]
                    run = tile[window - 8:]
                    for j in range(window // 8 - 2, -1, -1):
                        run = tile[j * 8:j * 8 + 8] + jnp.where(lanes8 >= 8, pltpu.roll(run, 8, 1), 0.0)
                    run = jnp.where(lanes8 >= rows8, pltpu.roll(run, 0, 1, stride=1, stride_axis=0), 0.0)
                    lines.append(jnp.sum(run, axis=0, keepdims=True))
            pred[chunk, q] = jnp.concatenate(lines, axis=0)
            if send:
                @pl.when(i < n_q - 1)
                def _():
                    p_copy(i + 1).start()
            return 0

        lax.fori_loop(0, n_q, body, 0)

    def p_copy(k):
        q = lax.rem(me_q + k, n_q)
        return pltpu.make_async_remote_copy(
            src_ref=pred.at[:, q], dst_ref=pred_got.at[k - 1], send_sem=p_send.at[k - 1], recv_sem=p_recv.at[k - 1],
            device_id={"sx": q // n_y, "sy": lax.rem(q, n_y)}, device_id_type=MESH)

    forward(mine, chunks == 1)
    for k in range(1, chunks):
        g_copy(k).wait_recv()
        forward(lax.rem(mine - k + chunks, chunks), k == chunks - 1)

    def finish(k, total):
        p_copy(k).wait_recv()
        return total + pred_got[k - 1]

    out_ref[...] = lax.fori_loop(1, n_q, finish, pred[:, me_q])

    def drain(k, _):
        p_copy(k).wait_send()
        return 0

    lax.fori_loop(1, n_q, drain, 0)
    for hop in range(1, n_s):
        s_copy((hop - 1) % chunks, hop).wait_send()
    for k in range(1, chunks):
        g_copy(k).wait_send()


def per_device(sizes, records, kernel_block, diffusion):
    vectors, sensors, window = records.shape
    cells_x, cells_y = diffusion.shape
    points = cells_x * cells_y
    n_s, n_x, n_y = sizes
    n_q = n_x * n_y
    chunks = min(n_s, vectors)
    per = vectors // chunks
    group = sensors // n_q
    margin, pairs, step = SWEEPS, cells_x // 2, 8
    kernel_rows = kernel_block.reshape(sensors, points, window)
    rates = jnp.broadcast_to(diffusion[None, :, :, None], (1, cells_x, cells_y, window))

    def halo_space(fields):
        return [
            pltpu.VMEM((2, fields, pairs, cells_y, window), F32),
            pltpu.VMEM((2, fields, margin, cells_y, window), F32),
            pltpu.VMEM((2, fields, pairs + margin, cells_y, window), F32),
            pltpu.VMEM((fields, cells_x + 2 * margin, 2 * cells_y, window), F32),
        ]

    dma = pltpu.SemaphoreType.DMA
    out = pl.pallas_call(
        functools.partial(kernel, sizes, vectors, sensors, cells_x, cells_y, window),
        out_shape=jax.ShapeDtypeStruct((chunks, per * group, window), F32),
        in_specs=[
            pl.BlockSpec(memory_space=pltpu.VMEM),
            pl.BlockSpec(memory_space=pltpu.VMEM),
            pl.BlockSpec(memory_space=pl.ANY),
        ],
        out_specs=pl.BlockSpec(memory_space=pltpu.VMEM),
        scratch_shapes=[
            pltpu.VMEM((sensors, points, window), BF16),
            pltpu.VMEM((vectors, sensors, window), F32),
            pltpu.VMEM((step * window, per * window), BF16),
            pltpu.VMEM((chunks, per, points, window), F32),
            pltpu.VMEM((max(n_s - 1, 1), per, points, window), F32),
            pltpu.VMEM((per, cells_x, cells_y, window), F32),
            *halo_space(per),
            *halo_space(1),
            pltpu.VMEM((chunks, per * window, points), BF16),
            pltpu.VMEM((chunks, n_q, per * group, window), F32),
            pltpu.VMEM((max(n_q - 1, 1), chunks, per * group, window), F32),
            dma((sensors // step,)),
            *[dma((max(n_s - 1, 1),))] * 2,
            *[dma((len(DIRECTIONS),))] * 4,
            *[dma((max(chunks - 1, 1),))] * 2,
            *[dma((max(n_q - 1, 1),))] * 2,
        ],
        compiler_params=pltpu.CompilerParams(collective_id=0, has_side_effects=True),
    )(records, rates, kernel_rows)
    return out.reshape(vectors, group, window)


def solution(mesh):
    sizes = tuple(mesh.shape[a] for a in ("sens", "sx", "sy"))
    return jax.shard_map(
        functools.partial(per_device, sizes),
        mesh=mesh,
        in_specs=(P(None, "sens", None), P("sens", "sx", "sy", None), P("sx", "sy")),
        out_specs=P(None, ("sens", "sx", "sy"), None),
        check_vma=False,
    )
```

time: 176 us -> 64.4 us (0.37)
  waiting for transfers between devices: 118 us -> 0 us
  Pallas kernels: 0 us -> 60.7 us
  starting transfers between devices: 20.2 us -> 0 us
  between operations: 14.3 us -> 0.01 us
  matrix products: 9.07 us -> 0 us
  local copies, waits for them, and re-layouts: 11.7 us -> 2.76 us
    unnamed x3 -> x0, waiting for transfers between devices: 89.8 us -> none
    pallas_call x0 -> x1, Pallas kernels: none -> 60.7 us  [per_device(): pl.pallas_call(functools.partial(kernel, sizes, vectors, sensors, cells_x...]
    psum x1 -> x0, waiting for transfers between devices: 23.8 us -> none  [per_device(): whole_sum = lax.psum(partials, 'sens')]
    ppermute x8 -> x0, starting transfers between devices: 20.2 us -> none  [the longest x4 15.1 us: extended(): before = lax.ppermute(last, axis, up)]
    conv_general_dilated x2 -> x0, matrix products: 9.07 us -> none  [the longest x1 6.13 us: per_device(): lax.conv_general_dilated(flipped, kernel_rows, (1,), [(0, window - 1)], d...]
    ppermute x8 -> x0, waiting for transfers between devices: 4.76 us -> none  [the longest x4 3.56 us: extended(): after = lax.ppermute(first, axis, down)]
    reshape x1 -> x0, local copies, waits for them, and re-layouts: 3.3 us -> none  [per_device(): kernel_rows = kernel.reshape(kernel.shape[0], cells_x * cells_y, window)]
    slice x4 -> x0, local copies, waits for them, and re-layouts: 1.78 us -> none  [the longest x3 0.9 us: extended(): last = lax.slice_in_dim(shard, length - width, length, axis=dim)]
  transfers between devices with their start and end apart: 10 -> 0, of which waited for: 5 -> 0; matrix products, arithmetic and copies ran while one was open for 6% -> 0% of each run, Pallas kernels for 0% -> 0%
where the time goes in v1:
time: 64.4 us; the launch traced here: 63.5 us
  Pallas kernels  60.7 us (94%)
  local copies, waits for them, and re-layouts  2.76 us (4%)
    pallas_call x1, Pallas kernels, per_device(): pl.pallas_call(functools.partial(kernel, sizes, vectors, sensors, cells_x...  60.7 us
    unnamed x2, local copies, waits for them, and re-layouts  2.05 us

profile of v1, /device:TPU:0, one launch (start us, length us, event | category | flops | bytes accessed | tf_op | source)
XLA Modules:
  0.0 63.5 jit_solution(16826749333247711613)
XLA Ops:
  0.0 0.8 %copy.4 = f32[16,8]{1,0:T(8,128)S(1)} copy(f32[16,8]{0,1:T(8,128)} %param.5) | data formatting | bytes 1024 | tf_op args[2]
  0.8 0.7 %broadcast_in_dim.2.rates_ref = f32[1,16,8,128]{3,2,1,0:T(8,128)} broadcast(f32[16,8]{1,0:T(8,128)S(1)} %copy.4), dimensions={1,2} | broadcast | bytes 66048 | tf_op jit(solution)/shard_map/broadcast_in_dim | solution.py:304
  1.5 60.7 %shard_map.37 = f32[2,8,128]{2,1,0:T(8,128)} custom-call(bf16[4,64,128]{2,1,0:T(8,128)(2,1)} %records_ref.1, f32[1,16,8,128]{3,2,1,0:T(8,128)} %broadcast_in_dim.2.rates_ref, bf16[64,128,128]{2,1,0:T(8,128)(2,1)} %bitcast.2), custom_call_target="tpu_custom_call" | custom-call | tf_op jit(solution)/shard_map/pallas_call | solution.py:315
  62.2 1.3 %copy.6 = f32[4,4,128]{2,1,0:T(4,128)} copy(f32[4,4,128]{2,1,0:T(4,128)} %bitcast.3) | data formatting | bytes 16384

commit v2 on v1

--- a/solution.py
+++ b/solution.py
@@ -239,28 +239,37 @@
 
     lanes8, rows8 = lane_iota(8, window), row_iota(8, window)
 
+    unroll = max(u for u in range(1, n_q + 1) if n_q % u == 0 and u * group <= 16)
+
     def forward(chunk, send):
         def body(i, _):
-            q = lax.rem(me_q + 1 + i, n_q)
-            rhs = jnp.concatenate([kbuf[q * group + s] for s in range(group)], axis=1)
-            res = jnp.dot(smooth_t[chunk], rhs, preferred_element_type=F32)
-            lines = []
-            for v in range(per):
-                for s in range(group):
-                    tile = res[v * window:(v + 1) * window, s * window:(s + 1) * window]
-                    run = tile[window - 8:]
-                    for j in range(window // 8 - 2, -1, -1):
-                        run = tile[j * 8:j * 8 + 8] + jnp.where(lanes8 >= 8, pltpu.roll(run, 8, 1), 0.0)
-                    run = jnp.where(lanes8 >= rows8, pltpu.roll(run, 0, 1, stride=1, stride_axis=0), 0.0)
-                    lines.append(jnp.sum(run, axis=0, keepdims=True))
-            pred[chunk, q] = jnp.concatenate(lines, axis=0)
+            for u in range(unroll):
+                q = lax.rem(me_q + 1 + i * unroll + u, n_q)
+                rhs = jnp.concatenate([kbuf[q * group + s] for s in range(group)], axis=1)
+                res = jnp.dot(smooth_t[chunk], rhs, preferred_element_type=F32)
+                lines = []
+                for v in range(per):
+                    for s in range(group):
+                        tile = res[v * window:(v + 1) * window, s * window:(s + 1) * window]
+                        terms = [tile[:8]]
+                        for j in range(1, window // 8):
+                            cut = jnp.where(lanes8 < window - 8 * j, tile[8 * j:8 * j + 8], 0.0)
+                            terms.append(pltpu.roll(cut, 8 * j, 1))
+                        while len(terms) > 1:
+                            terms = [a + b for a, b in zip(terms[::2], terms[1::2])]
+                        run = jnp.where(lanes8 >= rows8, pltpu.roll(terms[0], 0, 1, stride=1, stride_axis=0), 0.0)
+                        lines.append(jnp.sum(run, axis=0, keepdims=True))
+                pred[chunk, q] = jnp.concatenate(lines, axis=0)
             if send:
-                @pl.when(i < n_q - 1)
-                def _():
-                    p_copy(i + 1).start()
+                for u in range(unroll):
+                    k = i * unroll + u + 1
+
+                    @pl.when(k < n_q)
+                    def _():
+                        p_copy(k).start()
             return 0
 
-        lax.fori_loop(0, n_q, body, 0)
+        lax.fori_loop(0, n_q // unroll, body, 0)
 
     def p_copy(k):
         q = lax.rem(me_q + k, n_q)

time: 64.4 us -> 33.1 us (0.51); the launches traced: 63.5 us -> 32.9 us
  Pallas kernels: 60.7 us -> 30.1 us
    pallas_call x1, Pallas kernels: 60.7 us -> 30.1 us  [per_device(): pl.pallas_call(functools.partial(kernel, sizes, vectors, sensors, cells_x...]
where the time goes in v2:
time: 33.1 us; the launch traced here: 32.9 us
  Pallas kernels  30.1 us (91%)
  local copies, waits for them, and re-layouts  2.76 us (8%)
    pallas_call x1, Pallas kernels, per_device(): pl.pallas_call(functools.partial(kernel, sizes, vectors, sensors, cells_x...  30.1 us
    unnamed x2, local copies, waits for them, and re-layouts  2.05 us
    broadcast_in_dim x1, local copies, waits for them, and re-layouts, per_device(): jnp.broadcast_to(diffusion[None, :, :, None], (1, cells_x, cells_y, window))  0.7 us

profile of v2, /device:TPU:0, one launch (start us, length us, event | category | flops | bytes accessed | tf_op | source)
XLA Modules:
  0.0 32.9 jit_solution(17336845091770740825)
XLA Ops:
  0.0 0.8 %copy.4 = f32[16,8]{1,0:T(8,128)S(1)} copy(f32[16,8]{0,1:T(8,128)} %param.5) | data formatting | bytes 1024 | tf_op args[2]
  0.8 0.7 %broadcast_in_dim.2.rates_ref = f32[1,16,8,128]{3,2,1,0:T(8,128)} broadcast(f32[16,8]{1,0:T(8,128)S(1)} %copy.4), dimensions={1,2} | broadcast | bytes 66048 | tf_op jit(solution)/shard_map/broadcast_in_dim | solution.py:313
  1.5 30.1 %shard_map.37 = f32[2,8,128]{2,1,0:T(8,128)} custom-call(bf16[4,64,128]{2,1,0:T(8,128)(2,1)} %records_ref.1, f32[1,16,8,128]{3,2,1,0:T(8,128)} %broadcast_in_dim.2.rates_ref, bf16[64,128,128]{2,1,0:T(8,128)(2,1)} %bitcast.2), custom_call_target="tpu_custom_call" | custom-call | tf_op jit(solution)/shard_map/pallas_call | solution.py:324
  31.6 1.3 %copy.6 = f32[4,4,128]{2,1,0:T(4,128)} copy(f32[4,4,128]{2,1,0:T(4,128)} %bitcast.3) | data formatting | bytes 16384

commit v3 on v2

--- a/solution.py
+++ b/solution.py
@@ -96,24 +96,24 @@
         x_got[...] = jnp.zeros_like(x_got)
         y_got[...] = jnp.zeros_like(y_got)
 
-    def assemble(self, f, centre, x_got, y_got, wide):
+    def assemble(self, centre, x_got, y_got, wide):
         m, cx, cy = self.m, self.cx, self.cy
-        wide[f, pl.ds(m, cx), pl.ds(0, cy)] = centre[f]
-        wide[f, pl.ds(0, m), pl.ds(0, cy)] = x_got[0, f]
-        wide[f, pl.ds(m + cx, m), pl.ds(0, cy)] = x_got[1, f]
+        wide[0, pl.ds(m, cx), pl.ds(0, cy)] = centre[0]
+        wide[0, pl.ds(0, m), pl.ds(0, cy)] = x_got[0, 0]
+        wide[0, pl.ds(m + cx, m), pl.ds(0, cy)] = x_got[1, 0]
         upper = row_iota(cy, centre.shape[-1]) < cy // 2
         half = self.half
         first = [i - m for i in range(half)] + self.first + [cx + i for i in range(half)]
         second = [i - m + half for i in range(half)] + self.second + [cx + half + i for i in range(half)]
         for i, (a, b) in enumerate(zip(first, second)):
-            left, right = y_got[0, f, i], y_got[1, f, i]
-            wide[f, m + a, pl.ds(cy, cy)] = jnp.where(upper, right, left)
-            wide[f, m + b, pl.ds(cy, cy)] = pltpu.roll(jnp.where(upper, left, right), cy // 2, 0)
+            left, right = y_got[0, 0, i], y_got[1, 0, i]
+            wide[0, m + a, pl.ds(cy, cy)] = jnp.where(upper, right, left)
+            wide[0, m + b, pl.ds(cy, cy)] = pltpu.roll(jnp.where(upper, left, right), cy // 2, 0)
 
 
 def kernel(sizes, vectors, sensors, cells_x, cells_y, window,
-           records_ref, rates_ref, kernel_hbm, out_ref,
-           kbuf, recf, toep, part, got, field, packed, x_got, y_got, wide,
+           records_ref, rates_in, kernel_hbm, out_ref,
+           rates_ref, kbuf, recf, toep, part, got, field, packed, x_got, y_got, wide,
            d_packed, d_x_got, d_y_got, d_wide, smooth_t, pred, pred_got,
            k_sem, s_send, s_recv, h_send, h_recv, d_send, d_recv, g_send, g_recv, p_send, p_recv):
     n_s, n_x, n_y = sizes
@@ -156,6 +156,9 @@
     for v in range(vectors):
         recf[v] = jnp.dot(records_ref[v], anti, preferred_element_type=F32)
 
+    columns = rates_in[...]
+    for x in range(cells_x):
+        rates_ref[0, x] = jnp.broadcast_to(columns[:, x:x + 1], (cells_y, window))
     halo.pack(rates_ref, d_packed, 1)
 
     pack_rows = 16
@@ -186,40 +189,52 @@
 
         lax.fori_loop(0, steps, body, 0)
 
-    def s_copy(k, hop):
+    def s_copy(k, hop, v):
         return pltpu.make_async_remote_copy(
-            src_ref=part.at[k], dst_ref=got.at[hop - 1], send_sem=s_send.at[hop - 1], recv_sem=s_recv.at[hop - 1],
+            src_ref=part.at[k, v], dst_ref=got.at[hop - 1, v],
+            send_sem=s_send.at[hop - 1, v], recv_sem=s_recv.at[hop - 1, v],
             device_id={"sens": lax.rem(me_s + hop, n_s)}, device_id_type=MESH)
 
     halo_d = (rates_ref, d_packed, d_x_got, d_y_got, d_send, d_recv)
-    halo_f = (field, packed, x_got, y_got, h_send, h_recv)
+
+    def halo_f(v):
+        return tuple(ref.at[v] for ref in (field, packed, x_got, y_got, h_send, h_recv))
+
 
     for k in range(1, chunks + 1):
         adjoint(lax.rem(me_s + k, chunks), k - 1, k == 1)
         if k == 1:
             pl.semaphore_wait(barrier, n_q - 1 + n_s - 1)
-        for hop in range(k, n_s, chunks):
-            s_copy(k - 1, hop).start()
+        for v in range(per):
+            for hop in range(k, n_s, chunks):
+                s_copy(k - 1, hop, v).start()
         if k == 1:
             halo.start(*halo_d)
 
-    halo.wait(*halo_d)
-    halo.assemble(0, rates_ref, d_x_got, d_y_got, d_wide)
-
-    for hop in range(1, n_s):
-        s_copy((hop - 1) % chunks, hop).wait_recv()
     for v in range(per):
+        for hop in range(1, n_s):
+            s_copy((hop - 1) % chunks, hop, v).wait_recv()
         total = part[chunks - 1, v]
         for hop in range(1, n_s):
             total = total + got[hop - 1, v]
-        field[v] = total.reshape(cells_x, cells_y, window)
-    halo.pack(field, packed, per)
-    halo.start(*halo_f)
-    halo.wait(*halo_f)
+        field[v, 0] = total.reshape(cells_x, cells_y, window)
+        halo.pack(field.at[v], packed.at[v], 1)
+        halo.start(*halo_f(v))
+
+    halo.wait(*halo_d)
+    halo.assemble(rates_ref, d_x_got, d_y_got, d_wide)
+
+    def g_copy(k, v):
+        place = smooth_t.at[mine, pl.ds(v * window, window)]
+        return pltpu.make_async_remote_copy(
+            src_ref=place, dst_ref=place, send_sem=g_send.at[k - 1, v], recv_sem=g_recv.at[k - 1, v],
+            device_id={"sens": base + lax.rem(mine + k, chunks)}, device_id_type=MESH)
+
     wide_rows = 2 * cells_y
     for v in range(per):
-        halo.assemble(v, field, x_got, y_got, wide)
-        now = wide[v]
+        halo.wait(*halo_f(v))
+        halo.assemble(field.at[v], x_got.at[v], y_got.at[v], wide)
+        now = wide[0]
         for repeat in range(SWEEPS):
             interior = now[1:-1]
             beside = now[2:] + now[:-2] + pltpu.roll(interior, wide_rows - 1, 1) + pltpu.roll(interior, 1, 1)
@@ -228,20 +243,16 @@
         done = now[:, :cells_y].reshape(points, window).astype(BF16)
         smooth_t[mine, pl.ds(v * window, window)] = lax.dot_general(
             anti, done, (((1,), (1,)), ((), ())), preferred_element_type=F32).astype(BF16)
-
-    def g_copy(k):
-        return pltpu.make_async_remote_copy(
-            src_ref=smooth_t.at[mine], dst_ref=smooth_t.at[mine], send_sem=g_send.at[k - 1], recv_sem=g_recv.at[k - 1],
-            device_id={"sens": base + lax.rem(mine + k, chunks)}, device_id_type=MESH)
-
-    for k in range(1, chunks):
-        g_copy(k).start()
+        for k in range(1, chunks):
+            g_copy(k, v).start()
 
     lanes8, rows8 = lane_iota(8, window), row_iota(8, window)
 
     unroll = max(u for u in range(1, n_q + 1) if n_q % u == 0 and u * group <= 16)
 
-    def forward(chunk, send):
+    def forward(phase):
+        chunk = lax.rem(mine - phase + chunks, chunks)
+
         def body(i, _):
             for u in range(unroll):
                 q = lax.rem(me_q + 1 + i * unroll + u, n_q)
@@ -260,43 +271,47 @@
                         run = jnp.where(lanes8 >= rows8, pltpu.roll(terms[0], 0, 1, stride=1, stride_axis=0), 0.0)
                         lines.append(jnp.sum(run, axis=0, keepdims=True))
                 pred[chunk, q] = jnp.concatenate(lines, axis=0)
-            if send:
-                for u in range(unroll):
-                    k = i * unroll + u + 1
-
-                    @pl.when(k < n_q)
-                    def _():
-                        p_copy(k).start()
+            for u in range(unroll):
+                k = i * unroll + u + 1
+
+                @pl.when(k < n_q)
+                def _():
+                    p_copy(phase, k).start()
             return 0
 
         lax.fori_loop(0, n_q // unroll, body, 0)
 
-    def p_copy(k):
+    def p_copy(phase, k):
         q = lax.rem(me_q + k, n_q)
+        chunk = lax.rem(mine - phase + chunks, chunks)
         return pltpu.make_async_remote_copy(
-            src_ref=pred.at[:, q], dst_ref=pred_got.at[k - 1], send_sem=p_send.at[k - 1], recv_sem=p_recv.at[k - 1],
+            src_ref=pred.at[chunk, q], dst_ref=pred_got.at[k - 1, chunk],
+            send_sem=p_send.at[phase, k - 1], recv_sem=p_recv.at[phase, k - 1],
             device_id={"sx": q // n_y, "sy": lax.rem(q, n_y)}, device_id_type=MESH)
 
-    forward(mine, chunks == 1)
-    for k in range(1, chunks):
-        g_copy(k).wait_recv()
-        forward(lax.rem(mine - k + chunks, chunks), k == chunks - 1)
+    for phase in range(chunks):
+        for v in range(per if phase else 0):
+            g_copy(phase, v).wait_recv()
+        forward(phase)
 
     def finish(k, total):
-        p_copy(k).wait_recv()
+        for phase in range(chunks):
+            p_copy(phase, k).wait_recv()
         return total + pred_got[k - 1]
 
     out_ref[...] = lax.fori_loop(1, n_q, finish, pred[:, me_q])
 
     def drain(k, _):
-        p_copy(k).wait_send()
+        for phase in range(chunks):
+            p_copy(phase, k).wait_send()
         return 0
 
     lax.fori_loop(1, n_q, drain, 0)
-    for hop in range(1, n_s):
-        s_copy((hop - 1) % chunks, hop).wait_send()
-    for k in range(1, chunks):
-        g_copy(k).wait_send()
+    for v in range(per):
+        for hop in range(1, n_s):
+            s_copy((hop - 1) % chunks, hop, v).wait_send()
+        for k in range(1, chunks):
+            g_copy(k, v).wait_send()
 
 
 def per_device(sizes, records, kernel_block, diffusion):
@@ -310,14 +325,14 @@
     group = sensors // n_q
     margin, pairs, step = SWEEPS, cells_x // 2, 8
     kernel_rows = kernel_block.reshape(sensors, points, window)
-    rates = jnp.broadcast_to(diffusion[None, :, :, None], (1, cells_x, cells_y, window))
-
-    def halo_space(fields):
+    rates = diffusion.T
+
+    def halo_space(lead):
         return [
-            pltpu.VMEM((2, fields, pairs, cells_y, window), F32),
-            pltpu.VMEM((2, fields, margin, cells_y, window), F32),
-            pltpu.VMEM((2, fields, pairs + margin, cells_y, window), F32),
-            pltpu.VMEM((fields, cells_x + 2 * margin, 2 * cells_y, window), F32),
+            pltpu.VMEM((*lead, 2, 1, pairs, cells_y, window), F32),
+            pltpu.VMEM((*lead, 2, 1, margin, cells_y, window), F32),
+            pltpu.VMEM((*lead, 2, 1, pairs + margin, cells_y, window), F32),
+            pltpu.VMEM((1, cells_x + 2 * margin, 2 * cells_y, window), F32),
         ]
 
     dma = pltpu.SemaphoreType.DMA
@@ -331,22 +346,24 @@
         ],
         out_specs=pl.BlockSpec(memory_space=pltpu.VMEM),
         scratch_shapes=[
+            pltpu.VMEM((1, cells_x, cells_y, window), F32),
             pltpu.VMEM((sensors, points, window), BF16),
             pltpu.VMEM((vectors, sensors, window), F32),
             pltpu.VMEM((step * window, per * window), BF16),
             pltpu.VMEM((chunks, per, points, window), F32),
             pltpu.VMEM((max(n_s - 1, 1), per, points, window), F32),
-            pltpu.VMEM((per, cells_x, cells_y, window), F32),
-            *halo_space(per),
-            *halo_space(1),
+            pltpu.VMEM((per, 1, cells_x, cells_y, window), F32),
+            *halo_space((per,)),
+            *halo_space(()),
             pltpu.VMEM((chunks, per * window, points), BF16),
             pltpu.VMEM((chunks, n_q, per * group, window), F32),
             pltpu.VMEM((max(n_q - 1, 1), chunks, per * group, window), F32),
             dma((sensors // step,)),
-            *[dma((max(n_s - 1, 1),))] * 2,
-            *[dma((len(DIRECTIONS),))] * 4,
-            *[dma((max(chunks - 1, 1),))] * 2,
-            *[dma((max(n_q - 1, 1),))] * 2,
+            *[dma((max(n_s - 1, 1), per))] * 2,
+            *[dma((per, len(DIRECTIONS)))] * 2,
+            *[dma((len(DIRECTIONS),))] * 2,
+            *[dma((max(chunks - 1, 1), per))] * 2,
+            *[dma((chunks, max(n_q - 1, 1)))] * 2,
         ],
         compiler_params=pltpu.CompilerParams(collective_id=0, has_side_effects=True),
     )(records, rates, kernel_rows)

time: 33.1 us -> 30.5 us (0.921)
  local copies, waits for them, and re-layouts: 2.76 us -> 1.3 us
  Pallas kernels: 30.1 us -> 29 us
    pallas_call x1, Pallas kernels: 30.1 us -> 29 us  [per_device(): pl.pallas_call(functools.partial(kernel, sizes, vectors, sensors, cells_x...]
    unnamed x2 -> x1, local copies, waits for them, and re-layouts: 2.05 us -> 1.3 us
    broadcast_in_dim x1 -> x0, local copies, waits for them, and re-layouts: 0.7 us -> none  [per_device(): jnp.broadcast_to(diffusion[None, :, :, None], (1, cells_x, cells_y, window))]
where the time goes in v3:
time: 30.5 us; the launch traced here: 30.3 us
  Pallas kernels  29 us (95%)
  local copies, waits for them, and re-layouts  1.3 us (4%)
    pallas_call x1, Pallas kernels, per_device(): pl.pallas_call(functools.partial(kernel, sizes, vectors, sensors, cells_x...  29 us
    unnamed x1, local copies, waits for them, and re-layouts  1.3 us

profile of v3, /device:TPU:0, one launch (start us, length us, event | category | flops | bytes accessed | tf_op | source)
XLA Modules:
  0.0 30.3 jit_solution(1930918477662017340)
XLA Ops:
  0.0 29.0 %shard_map.37 = f32[2,8,128]{2,1,0:T(8,128)} custom-call(bf16[4,64,128]{2,1,0:T(8,128)(2,1)} %records_ref.1, f32[8,16]{1,0:T(8,128)} %bitcast.5, bf16[64,128,128]{2,1,0:T(8,128)(2,1)} %bitcast.3), custom_call_target="tpu_custom_call" | custom-call | tf_op jit(solution)/shard_map/pallas_call | solution.py:339
  29.0 1.3 %copy.5 = f32[4,4,128]{2,1,0:T(4,128)} copy(f32[4,4,128]{2,1,0:T(4,128)} %bitcast.4) | data formatting | bytes 16384

commit v4 on v3

--- a/solution.py
+++ b/solution.py
@@ -248,6 +248,17 @@
 
     lanes8, rows8 = lane_iota(8, window), row_iota(8, window)
 
+    bits = n_q.bit_length() - 1
+
+    def partner(k):
+        if n_q != 1 << bits:
+            return lax.rem(me_q + k, n_q)
+        total = 0
+        for b in range(bits):
+            one, two = lax.rem(me_q // (1 << b), 2), lax.rem(k // (1 << b), 2)
+            total = total + (one + two - 2 * one * two) * (1 << b)
+        return total
+
     unroll = max(u for u in range(1, n_q + 1) if n_q % u == 0 and u * group <= 16)
 
     def forward(phase):
@@ -255,7 +266,7 @@
 
         def body(i, _):
             for u in range(unroll):
-                q = lax.rem(me_q + 1 + i * unroll + u, n_q)
+                q = partner(n_q - 1 - (i * unroll + u))
                 rhs = jnp.concatenate([kbuf[q * group + s] for s in range(group)], axis=1)
                 res = jnp.dot(smooth_t[chunk], rhs, preferred_element_type=F32)
                 lines = []
@@ -272,9 +283,9 @@
                         lines.append(jnp.sum(run, axis=0, keepdims=True))
                 pred[chunk, q] = jnp.concatenate(lines, axis=0)
             for u in range(unroll):
-                k = i * unroll + u + 1
-
-                @pl.when(k < n_q)
+                k = n_q - 1 - (i * unroll + u)
+
+                @pl.when(k > 0)
                 def _():
                     p_copy(phase, k).start()
             return 0
@@ -282,7 +293,7 @@
         lax.fori_loop(0, n_q // unroll, body, 0)
 
     def p_copy(phase, k):
-        q = lax.rem(me_q + k, n_q)
+        q = partner(k)
         chunk = lax.rem(mine - phase + chunks, chunks)
         return pltpu.make_async_remote_copy(
             src_ref=pred.at[chunk, q], dst_ref=pred_got.at[k - 1, chunk],

time: 30.5 us -> 30.5 us (level)
  no operation moved by 1% of the time
where the time goes in v4:
time: 30.5 us; the launch traced here: 30.3 us
  Pallas kernels  29 us (95%)
  local copies, waits for them, and re-layouts  1.3 us (4%)
    pallas_call x1, Pallas kernels, per_device(): pl.pallas_call(functools.partial(kernel, sizes, vectors, sensors, cells_x...  29 us
    unnamed x1, local copies, waits for them, and re-layouts  1.3 us

profile of v4, /device:TPU:0, one launch (start us, length us, event | category | flops | bytes accessed | tf_op | source)
XLA Modules:
  0.0 30.3 jit_solution(5121167507083957504)
XLA Ops:
  0.0 29.0 %shard_map.37 = f32[2,8,128]{2,1,0:T(8,128)} custom-call(bf16[4,64,128]{2,1,0:T(8,128)(2,1)} %records_ref.1, f32[8,16]{1,0:T(8,128)} %bitcast.5, bf16[64,128,128]{2,1,0:T(8,128)(2,1)} %bitcast.3), custom_call_target="tpu_custom_call" | custom-call | tf_op jit(solution)/shard_map/pallas_call | solution.py:350
  29.0 1.3 %copy.5 = f32[4,4,128]{2,1,0:T(4,128)} copy(f32[4,4,128]{2,1,0:T(4,128)} %bitcast.4) | data formatting | bytes 16384
